TPU v7x, 512 devices: a whole 4x8x8 slice. The times are simulated.
512 devices in a mesh: row: 16 (over y, x_hi), col: 32 (over z, x_lo, core).
Axes of the slice: x: 4 (x_hi: 2, x_lo: 2; x = x_hi * 2 + x_lo), y: 8, z: 8, core: 2. Of those that a mesh axis runs over, the one named last changes fastest.
Arguments:
- sigma_anc: bfloat16 [4096, 4096], P('row', 'col'), as said below
- structure: int32 [512, 4], P(('row', 'col')), may hold values from 0 to 15, all different within a row
- factor: bfloat16 [512, 1024, 1024], P(('row', 'col')), may hold values from -0.375 to 0.375
- diag_term: float32 [512, 1024], P(('row', 'col')), may hold values from 1 to 8
Outputs:
- sigma_off: bfloat16 [512, 1024, 1024], P(('row', 'col'))
- variances: float32 [512, 1024], P(('row', 'col'))
Inputs may be any that keep to these rules, and one draw needn't show every extreme that they name: `structure`: each row names 4 different ancestor blocks, and every ancestor block is named by some row. sigma_anc is exactly symmetric, as the inverse of a symmetric precision matrix: its entry (p, q) equals its entry (q, p) bit for bit.
All inputs are finite; a program needn't handle non-finite values.
Results may differ from a plain program's by a relative error of at most 0.001.
Values may be sent and summed in bfloat16 or wider, within the bound.
No kernel may reach another device: no remote copies, remote signals or barrier semaphores. Data moves between devices by JAX's collectives and lax.ppermute only.
A program may use at most 64 MiB of HBM per device.

v0:
```python
import jax
import jax.numpy as jnp
from jax import lax
from jax.sharding import PartitionSpec as P


def body(sigma_anc, structure, factor, diag_term):
    span_count = structure.shape[1]
    block_rows = factor.shape[1] // span_count
    own_blocks = structure[0]
    triangle = factor[0]
    panel = lax.all_gather(sigma_anc, "col", axis=1, tiled=True)
    structures = lax.all_gather(structure, "row", axis=0, tiled=True)
    block_total = panel.shape[1] // block_rows
    blocked = panel.reshape(block_rows, block_total, block_rows)
    outgoing = jnp.take(blocked, structures, axis=1)
    outgoing = outgoing.reshape(block_rows, structures.shape[0], span_count * block_rows)
    received = lax.all_to_all(outgoing, "row", split_axis=1, concat_axis=1, tiled=True)
    picked = jnp.take(received, own_blocks, axis=1)
    product = jnp.einsum("bim,mw->ibw", picked, triangle, preferred_element_type=jnp.float32)
    off_block = -product.reshape(span_count * block_rows, triangle.shape[1])
    variance = diag_term[0] - jnp.sum(triangle.astype(jnp.float32) * off_block, axis=0)
    return (off_block.astype(jnp.bfloat16)[None], variance[None])


def solution(mesh):
    return jax.shard_map(
        body,
        mesh=mesh,
        in_specs=(
            P("row", "col"),
            P(("row", "col"), None),
            P(("row", "col"), None, None),
            P(("row", "col"), None),
        ),
        out_specs=(P(("row", "col"), None, None), P(("row", "col"), None)),
        check_vma=False,
    )
```

profile of v0, /device:TPU:17, one launch (start us, length us, event | category | flops | bytes accessed | tf_op | source)
XLA Modules:
  0.0 328.1 jit_solution(7711862939301773111)
XLA Ops:
  7.2 0.0 all-gather.3.cloned.1.call-start
  7.2 1.6 copy.21
  8.8 0.0 all-gather.3.cloned.1.call-update
  8.8 30.0 %all-gather = s32[16,1,4]{2,1,0:T(1,128)S(1)} all-gather(s32[1,1,4]{2,1,0:T(1,128)} %bitcast.47), channel_id=1, replica_groups=mesh['row'=16,'col'=32] {'row'}, dimensions={0}, use_global_device_ids=true | all-gather | bytes 272 | tf_op jit(solution)/shard_map/all_gather | solution.py:13
  38.8 0.1 copy.19
  38.9 0.1 copy.22
  39.0 0.1 reshape.70
  39.1 0.1 copy.20
  39.2 0.1 broadcast_in_dim.29
  39.3 43.8 %all-gather.3.cloned.1.call-done = bf16[256,4096]{0,1:T(8,128)(2,1)} async-done(((bf16[256,128]{0,1:T(8,128)(2,1)}), bf16[256,4096]{0,1:T(8,128)(2,1)}) %all-gather.3.cloned.1.call-update) | async-done | bytes 2097168 | tf_op jit(solution)/shard_map/all_gather | solution.py:12
  83.1 2.8 copy.23
  86.0 5.5 %gather_fusion = bf16[64,256,256]{2,1,0:T(8,128)(2,1)} fusion(bf16[256,16,256]{2,0,1:T(8,128)(2,1)S(1)} %copy.23, s32[1024]{0:T(1024)S(1)} %pad_clamp_fusion.1), kind=kCustom, calls=%fused_computation | custom fusion | bytes 16777472 | tf_op jit(solution)/shard_map/jit(_take)/gather | solution.py:16
  91.5 7.7 %copy.25 = bf16[16,4,32,8,256]{4,3,1,2,0:T(8,128)(2,1)} copy(bf16[16,4,32,8,256]{4,3,2,1,0:T(8,128)(2,1)} %bitcast.42) | data formatting | bytes 16777216 | tf_op jit(solution)/shard_map/jit(_take)/gather | solution.py:16
  99.1 7.4 %broadcast_select_fusion = bf16[256,16,1024]{2,0,1:T(8,128)(2,1)} fusion(bf16[256,16,1024]{2,0,1:T(8,128)(2,1)} %bitcast.41, pred[16,1024]{1,0:T(8,128)(4,1)S(1)} %bitcast.44), kind=kLoop, calls=%fused_computation.2 | loop fusion | flops 4194304 | bytes 16793600 | tf_op jit(solution)/shard_map/jit(_take)/select_n | solution.py:16
  106.5 0.0 copy-start.2
  106.5 9.0 %all-to-all-start = ((bf16[256,16,1024]{2,0,1:T(8,128)(2,1)}), bf16[256,16,1024]{2,0,1:T(8,128)(2,1)}, u32[]{:S(2)}, u32[]{:S(2)}) async-start(bf16[256,16,1024]{2,0,1:T(8,128)(2,1)} %broadcast_select_fusion), calls=%async_computation | async-start | bytes 16777216 | tf_op jit(solution)/shard_map/all_to_all | solution.py:18
  115.5 0.0 copy-done.2
  115.6 194.9 %all-to-all-done = bf16[256,16,1024]{2,0,1:T(8,128)(2,1)} async-done(((bf16[256,16,1024]{2,0,1:T(8,128)(2,1)}), bf16[256,16,1024]{2,0,1:T(8,128)(2,1)}, u32[]{:S(2)}, u32[]{:S(2)}) %all-to-all-start) | async-done | bytes 8388640 | tf_op jit(solution)/shard_map/all_to_all | solution.py:18
  310.4 4.1 %gather_fusion.1 = bf16[4,256,1024]{2,1,0:T(8,128)(2,1)S(1)} fusion(bf16[256,16,1024]{2,0,1:T(8,128)(2,1)} %all-to-all-done, s32[1024]{0:T(1024)S(1)} %pad_clamp_fusion), kind=kCustom, calls=%fused_computation.1 | custom fusion | bytes 4194320 | tf_op jit(solution)/shard_map/jit(_take)/gather | solution.py:19
  314.5 0.0 copy-start
  314.5 5.4 %fusion.8 = (bf16[256,4,1024]{2,0,1:T(8,128)(2,1)}, f32[256,4,1024]{2,0,1:T(8,128)S(1)}) fusion(bf16[1,1024,1024]{2,1,0:T(8,128)(2,1)} %param.6, bf16[4,256,1024]{2,1,0:T(8,128)(2,1)S(1)} %gather_fusion.1, pred[4]{0:T(512)(128)(4,1)S(1)} %compare_and_fusion.1), kind=kOutput, calls=%fused_computation.20 | convolution fusion | flops 2150629376 | bytes 10485764 | tf_op jit(solution)/shard_map/bim,mw->ibw/dot_general | solution.py:20
  319.9 0.0 copy-done
  319.9 0.0 copy-start.1
  319.9 0.5 fusion
  320.5 0.1 copy-done.1
  320.6 0.6 sub.4
  (7 shorter events, 0.0 us)
Async XLA Ops:
  7.2 75.9 %all-gather.3.cloned.1.call-start = ((), (), s32[]{:S(2)}) async-start(), calls=%async_computation.1 | async-start | bytes 2162688 | tf_op jit(solution)/shard_map/all_gather | solution.py:12
  106.5 9.0 %copy-start.2 = (s32[1,4]{1,0:T(1,128)S(1)}, s32[1,4]{1,0:T(1,128)}, u32[]{:S(2)}) copy-start(s32[1,4]{1,0:T(1,128)} %param.5) | copy-start | bytes 52
  106.5 203.9 %all-to-all-start = ((bf16[256,16,1024]{2,0,1:T(8,128)(2,1)}), bf16[256,16,1024]{2,0,1:T(8,128)(2,1)}, u32[]{:S(2)}, u32[]{:S(2)}) async-start(bf16[256,16,1024]{2,0,1:T(8,128)(2,1)} %broadcast_select_fusion), calls=%async_computation | async-start | bytes 16777216 | tf_op jit(solution)/shard_map/all_to_all | solution.py:18
  314.5 5.4 %copy-start = (bf16[1,1024,1024]{2,1,0:T(8,128)(2,1)S(1)}, bf16[1,1024,1024]{2,1,0:T(8,128)(2,1)}, u32[]{:S(2)}) copy-start(bf16[1,1024,1024]{2,1,0:T(8,128)(2,1)} %param.6) | copy-start | bytes 6291460
  319.9 0.7 copy-start.1
Sparse Core Ops, SparseCore 0:
  10.7 72.3 all-gather.2
where the time goes:
time: 329 us; the launch traced here: 328 us
  waiting for transfers between devices  239 us (73%)
  blocking collectives  30 us (9%)
  local copies, waits for them, and re-layouts  22.3 us (7%)
  between operations  14.1 us (4%)
  starting transfers between devices  9.01 us (3%)
  other arithmetic  8.57 us (3%)
  matrix products  5.43 us (2%)
    all_to_all x1, waiting for transfers between devices, body(): lax.all_to_all(outgoing, 'row', split_axis=1, concat_axis=1, tiled=True)  195 us
    all_gather x1, waiting for transfers between devices, body(): panel = lax.all_gather(sigma_anc, 'col', axis=1, tiled=True)  43.8 us
    all_gather x1, blocking collectives, body(): structures = lax.all_gather(structure, 'row', axis=0, tiled=True)  30 us
    gather x2, local copies, waits for them, and re-layouts, body(): outgoing = jnp.take(blocked, structures, axis=1)  13.2 us
    all_to_all x1, starting transfers between devices, body(): lax.all_to_all(outgoing, 'row', split_axis=1, concat_axis=1, tiled=True)  8.97 us
    select_n x2, other arithmetic, body(): outgoing = jnp.take(blocked, structures, axis=1)  7.4 us
  transfers between devices with their start and end apart: 2, of which 2 were waited for; matrix products, arithmetic and copies ran while one was open for 0% of the time, Pallas kernels for 0%

commit v1 on v0

--- a/solution.py
+++ b/solution.py
@@ -9,7 +9,8 @@
     block_rows = factor.shape[1] // span_count
     own_blocks = structure[0]
     triangle = factor[0]
-    panel = lax.all_gather(sigma_anc, "col", axis=1, tiled=True)
+    stack = jnp.stack([sigma_anc] * lax.axis_size("col"))
+    panel = jnp.concatenate(lax.all_to_all(stack, "col", 0, 0), axis=1)
     structures = lax.all_gather(structure, "row", axis=0, tiled=True)
     block_total = panel.shape[1] // block_rows
     blocked = panel.reshape(block_rows, block_total, block_rows)

time: 329 us -> 306 us (0.930)
  the two profiles are of different devices: /device:TPU:17 before, /device:TPU:23 now
where the time goes in v1:
time: 306 us; the launch traced here: 305 us
  waiting for transfers between devices  214 us (70%)
  blocking collectives  30.4 us (10%)
  local copies, waits for them, and re-layouts  24.6 us (8%)
  starting transfers between devices  21.6 us (7%)
  other arithmetic  8.57 us (3%)
  matrix products  5.43 us (2%)
    all_to_all x1, waiting for transfers between devices, body(): lax.all_to_all(outgoing, 'row', split_axis=1, concat_axis=1, tiled=True)  195 us
    all_gather x1, blocking collectives, body(): structures = lax.all_gather(structure, 'row', axis=0, tiled=True)  30.4 us
    all_to_all x1, waiting for transfers between devices, body(): panel = jnp.concatenate(lax.all_to_all(stack, 'col', 0, 0), axis=1)  19.2 us
    gather x2, local copies, waits for them, and re-layouts, body(): outgoing = jnp.take(blocked, structures, axis=1)  13.2 us
    all_to_all x1, starting transfers between devices, body(): panel = jnp.concatenate(lax.all_to_all(stack, 'col', 0, 0), axis=1)  12.3 us
    all_to_all x1, starting transfers between devices, body(): lax.all_to_all(outgoing, 'row', split_axis=1, concat_axis=1, tiled=True)  9.29 us
    select_n x2, other arithmetic, body(): outgoing = jnp.take(blocked, structures, axis=1)  7.4 us
  transfers between devices with their start and end apart: 2, of which 2 were waited for; matrix products, arithmetic and copies ran while one was open for 0% of the time, Pallas kernels for 0%

profile of v1, /device:TPU:23, one launch (start us, length us, event | category | flops | bytes accessed | tf_op | source)
XLA Modules:
  0.0 305.3 jit_solution(8509128801347750438)
XLA Ops:
  0.6 0.9 copy.17
  1.6 1.6 stack.2
  3.1 0.0 copy-start.3
  3.1 12.3 %all-to-all-start = ((bf16[32,256,128]{1,2,0:T(8,128)(2,1)}), bf16[32,256,128]{1,2,0:T(8,128)(2,1)S(1)}, u32[]{:S(2)}, u32[]{:S(2)}) async-start(bf16[32,256,128]{1,2,0:T(8,128)(2,1)} %stack.2), calls=%async_computation | async-start | bytes 4194304 | tf_op jit(solution)/shard_map/all_to_all | solution.py:13
  15.5 0.0 copy-done.3
  15.5 30.4 %all-gather = s32[16,1,4]{2,1,0:T(1,128)S(1)} all-gather(s32[1,1,4]{2,1,0:T(1,128)S(1)} %bitcast.49), channel_id=1, replica_groups=mesh['row'=16,'col'=32] {'row'}, dimensions={0}, use_global_device_ids=true | all-gather | bytes 272 | tf_op jit(solution)/shard_map/all_gather | solution.py:14
  45.8 0.1 copy.15
  45.9 0.1 copy.18
  46.0 0.1 reshape.72
  46.1 0.1 copy.16
  46.2 0.1 broadcast_in_dim.29
  46.4 19.2 %all-to-all-done = bf16[32,256,128]{1,2,0:T(8,128)(2,1)S(1)} async-done(((bf16[32,256,128]{1,2,0:T(8,128)(2,1)}), bf16[32,256,128]{1,2,0:T(8,128)(2,1)S(1)}, u32[]{:S(2)}, u32[]{:S(2)}) %all-to-all-start) | async-done | bytes 2097184 | tf_op jit(solution)/shard_map/all_to_all | solution.py:13
  65.6 0.0 copy-start
  65.6 1.3 copy-done
  66.9 2.8 copy.19
  69.8 5.5 %gather_fusion = bf16[64,256,256]{2,1,0:T(8,128)(2,1)} fusion(bf16[256,16,256]{2,0,1:T(8,128)(2,1)S(1)} %copy.19, s32[1024]{0:T(1024)S(1)} %pad_clamp_fusion.1), kind=kCustom, calls=%fused_computation | custom fusion | bytes 16777472 | tf_op jit(solution)/shard_map/jit(_take)/gather | solution.py:17
  75.3 7.7 %copy.21 = bf16[16,4,32,8,256]{4,3,1,2,0:T(8,128)(2,1)} copy(bf16[16,4,32,8,256]{4,3,2,1,0:T(8,128)(2,1)} %bitcast.44) | data formatting | bytes 16777216 | tf_op jit(solution)/shard_map/jit(_take)/gather | solution.py:17
  83.0 7.4 %broadcast_select_fusion = bf16[256,16,1024]{2,0,1:T(8,128)(2,1)} fusion(bf16[256,16,1024]{2,0,1:T(8,128)(2,1)} %bitcast.43, pred[16,1024]{1,0:T(8,128)(4,1)S(1)} %bitcast.46), kind=kLoop, calls=%fused_computation.2 | loop fusion | flops 4194304 | bytes 16793600 | tf_op jit(solution)/shard_map/jit(_take)/select_n | solution.py:17
  90.4 9.3 %all-to-all-start.1 = ((bf16[256,16,1024]{2,0,1:T(8,128)(2,1)}), bf16[256,16,1024]{2,0,1:T(8,128)(2,1)}, u32[]{:S(2)}, u32[]{:S(2)}) async-start(bf16[256,16,1024]{2,0,1:T(8,128)(2,1)} %broadcast_select_fusion), calls=%async_computation.1 | async-start | bytes 16777216 | tf_op jit(solution)/shard_map/all_to_all | solution.py:19
  99.7 194.8 %all-to-all-done.1 = bf16[256,16,1024]{2,0,1:T(8,128)(2,1)} async-done(((bf16[256,16,1024]{2,0,1:T(8,128)(2,1)}), bf16[256,16,1024]{2,0,1:T(8,128)(2,1)}, u32[]{:S(2)}, u32[]{:S(2)}) %all-to-all-start.1) | async-done | bytes 8388640 | tf_op jit(solution)/shard_map/all_to_all | solution.py:19
  294.5 4.1 %gather_fusion.1 = bf16[4,256,1024]{2,1,0:T(8,128)(2,1)S(1)} fusion(bf16[256,16,1024]{2,0,1:T(8,128)(2,1)} %all-to-all-done.1, s32[1024]{0:T(1024)S(1)} %pad_clamp_fusion), kind=kCustom, calls=%fused_computation.1 | custom fusion | bytes 4194320 | tf_op jit(solution)/shard_map/jit(_take)/gather | solution.py:20
  298.6 0.0 copy-start.1
  298.6 5.4 %fusion.8 = (bf16[256,4,1024]{2,0,1:T(8,128)(2,1)}, f32[256,4,1024]{2,0,1:T(8,128)S(1)}) fusion(bf16[1,1024,1024]{2,1,0:T(8,128)(2,1)} %param.6, bf16[4,256,1024]{2,1,0:T(8,128)(2,1)S(1)} %gather_fusion.1, pred[4]{0:T(512)(128)(4,1)S(1)} %compare_and_fusion.1), kind=kOutput, calls=%fused_computation.20 | convolution fusion | flops 2150629376 | bytes 10485764 | tf_op jit(solution)/shard_map/bim,mw->ibw/dot_general | solution.py:21
  304.0 0.0 copy-done.1
  304.0 0.0 copy-start.2
  304.0 0.5 fusion
  304.6 0.1 copy-done.2
  304.7 0.6 sub.4
  (7 shorter events, 0.0 us)
Async XLA Ops:
  3.1 12.4 %copy-start.3 = (s32[1,4]{1,0:T(1,128)S(1)}, s32[1,4]{1,0:T(1,128)}, u32[]{:S(2)}) copy-start(s32[1,4]{1,0:T(1,128)} %param.5) | copy-start | bytes 52
  3.1 62.5 %all-to-all-start = ((bf16[32,256,128]{1,2,0:T(8,128)(2,1)}), bf16[32,256,128]{1,2,0:T(8,128)(2,1)S(1)}, u32[]{:S(2)}, u32[]{:S(2)}) async-start(bf16[32,256,128]{1,2,0:T(8,128)(2,1)} %stack.2), calls=%async_computation | async-start | bytes 4194304 | tf_op jit(solution)/shard_map/all_to_all | solution.py:13
  65.6 1.3 copy-start
  90.4 204.1 %all-to-all-start.1 = ((bf16[256,16,1024]{2,0,1:T(8,128)(2,1)}), bf16[256,16,1024]{2,0,1:T(8,128)(2,1)}, u32[]{:S(2)}, u32[]{:S(2)}) async-start(bf16[256,16,1024]{2,0,1:T(8,128)(2,1)} %broadcast_select_fusion), calls=%async_computation.1 | async-start | bytes 16777216 | tf_op jit(solution)/shard_map/all_to_all | solution.py:19
  298.6 5.4 %copy-start.1 = (bf16[1,1024,1024]{2,1,0:T(8,128)(2,1)S(1)}, bf16[1,1024,1024]{2,1,0:T(8,128)(2,1)}, u32[]{:S(2)}) copy-start(bf16[1,1024,1024]{2,1,0:T(8,128)(2,1)} %param.6) | copy-start | bytes 6291460
  304.0 0.7 copy-start.2
